TPU v7x, 32 devices: a whole 2x2x4 slice. The times are simulated.
32 devices in a mesh: wide: 8 (over y, x, core), narrow: 4 (over z).
Axes of the slice: x: 2, y: 2, z: 4, core: 2. Of those that a mesh axis runs over, the one named last changes fastest.
Arguments:
- hidden_in: bfloat16 [16, 1024, 768], P('wide', 'narrow'), may hold values from -6 to 6
- positions: int32 [16, 1024], P('wide', 'narrow'), may hold values from 0 to 1023, as said below
- time_index: int32 [16], P('wide'), may hold values from 0 to 1023
- cond_table: bfloat16 [1024, 128], replicated, may hold values from -5 to 5
- ada_weight: bfloat16 [128, 4608], replicated, may hold values from -0.5 to 0.5
- norm1_gain: bfloat16 [768], replicated, may hold values from 0.099609375 to 1.8984375
- qkv_weight: bfloat16 [768, 2304], replicated, may hold values from -0.21875 to 0.21875
- out_weight: bfloat16 [768, 768], replicated, may hold values from -0.875 to 0.875
- norm2_gain: bfloat16 [768], replicated, may hold values from 0.099609375 to 1.8984375
- up_weight: bfloat16 [768, 3072], replicated, may hold values from -0.21875 to 0.21875
- down_weight: bfloat16 [3072, 768], replicated, may hold values from -0.21875 to 0.21875
- cotangent: bfloat16 [16, 1024, 768], P('wide', 'narrow'), may hold values from -6 to 6
Outputs:
- hidden_out: bfloat16 [16, 1024, 768], P('wide', 'narrow')
- hidden_grad: bfloat16 [16, 1024, 768], P('wide', 'narrow')
- cond_table_grad: float32 [1024, 128], P('wide', 'narrow')
- ada_weight_grad: float32 [128, 4608], P('narrow', 'wide')
- norm1_gain_grad: float32 [768], P('wide')
- qkv_weight_grad: float32 [768, 2304], P('wide', 'narrow')
- out_weight_grad: float32 [768, 768], P('wide', 'narrow')
- norm2_gain_grad: float32 [768], P('wide')
- up_weight_grad: float32 [768, 3072], P('wide', 'narrow')
- down_weight_grad: float32 [3072, 768], P('wide', 'narrow')
Inputs may be any that keep to these rules, and one draw needn't show every extreme that they name: positions count up by one from the start of each packed document, every row starts a document at its first token, and one row is a single document.
All inputs are finite; a program needn't handle non-finite values.
Results may differ from a plain program's by a relative error of at most 0.015.
The roundings to bfloat16 on the way count: a program that leaves them out, or rounds other values in their place, can miss the bound.
Values may be sent and summed in bfloat16 or wider, within the bound.
No kernel may reach another device: no remote copies, remote signals or barrier semaphores. Data moves between devices by JAX's collectives and lax.ppermute only.
A program may use at most 192 MiB of HBM per device.

v0:
```python
import jax
import jax.numpy as jnp
from jax import lax
from jax.sharding import PartitionSpec as P

HEAD_DIM = 64
HIGHEST = lax.Precision.HIGHEST
norm_eps = 1e-05


def norm_mod(hidden, gain, shift, scale):
    center = hidden - jnp.mean(hidden, axis=-1, keepdims=True)
    variance = jnp.mean(center * center, axis=-1, keepdims=True)
    return center * lax.rsqrt(variance + norm_eps) * gain * (1.0 + scale) + shift


def rotary(values, positions):
    half_dim = values.shape[-1] // 2
    frequency = 10000.0 ** (-jnp.arange(half_dim, dtype=jnp.float32) / half_dim)
    angles = positions.astype(jnp.float32)[..., None, None] * frequency
    cosine = jnp.cos(angles)
    sine = jnp.sin(angles)
    first_half = values[..., :half_dim]
    second_half = values[..., half_dim:]
    return jnp.concatenate(
        [first_half * cosine - second_half * sine, second_half * cosine + first_half * sine],
        axis=-1,
    )


def gelu_tanh(values):
    return jax.nn.gelu(values, approximate=True)


def tdot(left, right):
    return lax.dot_general(
        left, right, (((0,), (0,)), ((), ())), preferred_element_type=jnp.float32
    )


def ndot(left, right):
    return lax.dot_general(
        left, right, (((1,), (1,)), ((), ())), preferred_element_type=jnp.float32
    )


def attend(row_item):
    queries, key_rows, value_rows = row_item
    length = queries.shape[0]
    local_heads = queries.shape[1] // HEAD_DIM
    queries = queries.reshape(length, local_heads, HEAD_DIM)
    key_rows = key_rows.reshape(length, local_heads, HEAD_DIM)
    value_rows = value_rows.reshape(length, local_heads, HEAD_DIM)
    scores = jnp.einsum(
        "qhd,khd->hqk", queries, key_rows, preferred_element_type=jnp.float32
    ) * HEAD_DIM ** (-0.5)
    row_max = jnp.max(scores, axis=-1, keepdims=True)
    expo = jnp.exp(scores - row_max)
    row_total = jnp.sum(expo, axis=-1, keepdims=True)
    probs = expo / row_total
    log_total = row_max + jnp.log(row_total)
    result = jnp.einsum(
        "hqk,khd->qhd", probs.astype(jnp.bfloat16), value_rows, preferred_element_type=jnp.float32
    )
    return (result.astype(jnp.bfloat16).reshape(length, local_heads * HEAD_DIM), log_total)


def attend_back(row_item):
    queries, key_rows, value_rows, d_result, log_total = row_item
    length = queries.shape[0]
    local_heads = queries.shape[1] // HEAD_DIM
    queries = queries.reshape(length, local_heads, HEAD_DIM)
    key_rows = key_rows.reshape(length, local_heads, HEAD_DIM)
    value_rows = value_rows.reshape(length, local_heads, HEAD_DIM)
    d_result = d_result.reshape(length, local_heads, HEAD_DIM)
    score_scale = HEAD_DIM ** (-0.5)
    scores = (
        jnp.einsum("qhd,khd->hqk", queries, key_rows, preferred_element_type=jnp.float32)
        * score_scale
    )
    probs = jnp.exp(scores - log_total)
    d_values = jnp.einsum(
        "hqk,qhd->khd", probs.astype(jnp.bfloat16), d_result, preferred_element_type=jnp.float32
    )
    d_probs = jnp.einsum("qhd,khd->hqk", d_result, value_rows, preferred_element_type=jnp.float32)
    d_scores = probs * (d_probs - jnp.sum(probs * d_probs, axis=-1, keepdims=True))
    d_low = d_scores.astype(jnp.bfloat16)
    d_queries = (
        jnp.einsum("hqk,khd->qhd", d_low, key_rows, preferred_element_type=jnp.float32)
        * score_scale
    )
    d_keys = (
        jnp.einsum("hqk,qhd->khd", d_low, queries, preferred_element_type=jnp.float32) * score_scale
    )
    width_local = local_heads * HEAD_DIM
    return (
        d_queries.astype(jnp.bfloat16).reshape(length, width_local),
        d_keys.astype(jnp.bfloat16).reshape(length, width_local),
        d_values.astype(jnp.bfloat16).reshape(length, width_local),
    )


def blocks_rows_wide(grad, wide_count, narrow_count):
    rows, cols = grad.shape
    split = grad.reshape(wide_count, rows // wide_count, narrow_count, cols // narrow_count)
    return split.transpose(0, 2, 1, 3).reshape(wide_count, narrow_count, -1)


def blocks_rows_narrow(grad, wide_count, narrow_count):
    rows, cols = grad.shape
    split = grad.reshape(narrow_count, rows // narrow_count, wide_count, cols // wide_count)
    return split.transpose(2, 0, 1, 3).reshape(wide_count, narrow_count, -1)


def blocks_gain(grad, wide_count, narrow_count):
    split = grad.reshape(wide_count, 1, grad.shape[0] // wide_count)
    return jnp.broadcast_to(split, (wide_count, narrow_count, grad.shape[0] // wide_count))


def on_device(
    hidden_in,
    positions,
    time_index,
    cond_table,
    ada_weight,
    norm1_gain,
    qkv_weight,
    out_weight,
    norm2_gain,
    up_weight,
    down_weight,
    cotangent,
):
    row_count, part_len, model_width = hidden_in.shape
    tokens = row_count * part_len
    heads_all = model_width // HEAD_DIM
    times = cond_table.shape[0]
    onehot = (time_index[:, None] == jnp.arange(times, dtype=jnp.int32)[None, :]).astype(
        jnp.float32
    )
    embedded = jnp.dot(
        onehot,
        cond_table.astype(jnp.float32),
        precision=HIGHEST,
        preferred_element_type=jnp.float32,
    )
    condition_low = jax.nn.silu(embedded).astype(jnp.bfloat16)
    modulation = jnp.dot(condition_low, ada_weight, preferred_element_type=jnp.float32)
    pieces = [
        modulation[:, None, index * model_width : (index + 1) * model_width] for index in range(6)
    ]
    shift_one, scale_one, gate_one, shift_two, scale_two, gate_two = pieces
    hidden_full = hidden_in.astype(jnp.float32)
    gain_one = norm1_gain.astype(jnp.float32)
    gain_two = norm2_gain.astype(jnp.float32)
    norm_one = (
        norm_mod(hidden_full, gain_one, shift_one, scale_one)
        .astype(jnp.bfloat16)
        .reshape(tokens, model_width)
    )
    qkv = jnp.dot(norm_one, qkv_weight, preferred_element_type=jnp.float32).reshape(
        row_count, part_len, 3, heads_all, HEAD_DIM
    )
    query_pre = qkv[:, :, 0]
    key_pre = qkv[:, :, 1]
    query_low = (
        rotary(query_pre, positions).astype(jnp.bfloat16).reshape(row_count, part_len, model_width)
    )
    key_low = (
        rotary(key_pre, positions).astype(jnp.bfloat16).reshape(row_count, part_len, model_width)
    )
    value_low = qkv[:, :, 2].astype(jnp.bfloat16).reshape(row_count, part_len, model_width)
    query_heads, key_heads, value_heads = (
        lax.all_to_all(query_low, "narrow", split_axis=2, concat_axis=1, tiled=True),
        lax.all_to_all(key_low, "narrow", split_axis=2, concat_axis=1, tiled=True),
        lax.all_to_all(value_low, "narrow", split_axis=2, concat_axis=1, tiled=True),
    )
    attended_heads, log_totals = lax.map(attend, (query_heads, key_heads, value_heads))
    attended = lax.all_to_all(
        attended_heads, "narrow", split_axis=1, concat_axis=2, tiled=True
    ).reshape(tokens, model_width)
    projected = jnp.dot(attended, out_weight, preferred_element_type=jnp.float32).reshape(
        row_count, part_len, model_width
    )
    middle = hidden_full + gate_one * projected
    norm_two = (
        norm_mod(middle, gain_two, shift_two, scale_two)
        .astype(jnp.bfloat16)
        .reshape(tokens, model_width)
    )
    up_part = jnp.dot(norm_two, up_weight, preferred_element_type=jnp.float32)
    activated = gelu_tanh(up_part).astype(jnp.bfloat16)
    down_part = jnp.dot(activated, down_weight, preferred_element_type=jnp.float32).reshape(
        row_count, part_len, model_width
    )
    hidden_out = (middle + gate_two * down_part).astype(jnp.bfloat16)
    d_out = cotangent.astype(jnp.float32)
    d_gate_two = jnp.sum(d_out * down_part, axis=1)
    d_down = (d_out * gate_two).astype(jnp.bfloat16).reshape(tokens, model_width)
    grad_down = tdot(activated, d_down)
    d_activated = ndot(d_down, down_weight)
    unused_gelu, gelu_back = jax.vjp(gelu_tanh, up_part)
    d_up = gelu_back(d_activated)[0].astype(jnp.bfloat16)
    grad_up = tdot(norm_two, d_up)
    d_norm_two = ndot(d_up, up_weight).reshape(row_count, part_len, model_width)
    unused_two, norm_two_back = jax.vjp(norm_mod, middle, gain_two, shift_two, scale_two)
    d_middle_norm, grad_gain_two, d_shift_two, d_scale_two = norm_two_back(d_norm_two)
    d_middle = d_out + d_middle_norm
    d_gate_one = jnp.sum(d_middle * projected, axis=1)
    d_projected = (d_middle * gate_one).astype(jnp.bfloat16).reshape(tokens, model_width)
    grad_out = tdot(attended, d_projected)
    d_attended = (
        ndot(d_projected, out_weight).astype(jnp.bfloat16).reshape(row_count, part_len, model_width)
    )
    d_attended_heads = lax.all_to_all(d_attended, "narrow", split_axis=2, concat_axis=1, tiled=True)
    d_query_heads, d_key_heads, d_value_heads = lax.map(
        attend_back, (query_heads, key_heads, value_heads, d_attended_heads, log_totals)
    )
    d_query, d_key, d_value = (
        lax.all_to_all(d_query_heads, "narrow", split_axis=1, concat_axis=2, tiled=True),
        lax.all_to_all(d_key_heads, "narrow", split_axis=1, concat_axis=2, tiled=True),
        lax.all_to_all(d_value_heads, "narrow", split_axis=1, concat_axis=2, tiled=True),
    )

    def rotate_both(query_part, key_part):
        return (rotary(query_part, positions), rotary(key_part, positions))

    unused_rot, rotate_back = jax.vjp(rotate_both, query_pre, key_pre)
    head_shape = (row_count, part_len, heads_all, HEAD_DIM)
    d_query_pre, d_key_pre = rotate_back(
        (
            d_query.astype(jnp.float32).reshape(head_shape),
            d_key.astype(jnp.float32).reshape(head_shape),
        )
    )
    d_qkv = jnp.stack(
        [d_query_pre, d_key_pre, d_value.astype(jnp.float32).reshape(head_shape)], axis=2
    )
    d_qkv = d_qkv.astype(jnp.bfloat16).reshape(tokens, 3 * model_width)
    grad_qkv = tdot(norm_one, d_qkv)
    d_norm_one = ndot(d_qkv, qkv_weight).reshape(row_count, part_len, model_width)
    unused_one, norm_one_back = jax.vjp(norm_mod, hidden_full, gain_one, shift_one, scale_one)
    d_hidden_norm, grad_gain_one, d_shift_one, d_scale_one = norm_one_back(d_norm_one)
    hidden_grad = (d_middle + d_hidden_norm).astype(jnp.bfloat16)
    d_modulation = jnp.concatenate(
        [
            d_shift_one.reshape(row_count, model_width),
            d_scale_one.reshape(row_count, model_width),
            d_gate_one,
            d_shift_two.reshape(row_count, model_width),
            d_scale_two.reshape(row_count, model_width),
            d_gate_two,
        ],
        axis=1,
    )
    grad_ada = lax.dot_general(
        condition_low.astype(jnp.float32),
        d_modulation,
        (((0,), (0,)), ((), ())),
        precision=HIGHEST,
        preferred_element_type=jnp.float32,
    )
    d_condition = lax.dot_general(
        d_modulation,
        ada_weight.astype(jnp.float32),
        (((1,), (1,)), ((), ())),
        precision=HIGHEST,
        preferred_element_type=jnp.float32,
    )
    unused_silu, silu_back = jax.vjp(jax.nn.silu, embedded)
    d_embedded = silu_back(d_condition)[0]
    grad_table = lax.dot_general(
        onehot,
        d_embedded,
        (((0,), (0,)), ((), ())),
        precision=HIGHEST,
        preferred_element_type=jnp.float32,
    )
    wide_count = lax.axis_size("wide")
    narrow_count = lax.axis_size("narrow")
    weight_grads = [
        grad_table,
        grad_ada,
        grad_gain_one,
        grad_qkv,
        grad_out,
        grad_gain_two,
        grad_up,
        grad_down,
    ]
    kinds = ["wide", "narrow", "gain", "wide", "wide", "gain", "wide", "wide"]
    block_list = []
    local_shapes = []
    for item, kind in zip(weight_grads, kinds):
        if kind == "wide":
            block_list.append(blocks_rows_wide(item, wide_count, narrow_count))
            local_shapes.append((item.shape[0] // wide_count, item.shape[1] // narrow_count))
        elif kind == "narrow":
            block_list.append(blocks_rows_narrow(item, wide_count, narrow_count))
            local_shapes.append((item.shape[0] // narrow_count, item.shape[1] // wide_count))
        else:
            block_list.append(blocks_gain(item, wide_count, narrow_count))
            local_shapes.append((item.shape[0] // wide_count,))
    stacked = jnp.concatenate(block_list, axis=2)
    joined = stacked.reshape(wide_count * narrow_count, stacked.shape[2])
    summed = lax.psum_scatter(joined, ("wide", "narrow"), scatter_dimension=0, tiled=True).reshape(
        -1
    )
    results = []
    offset = 0
    for shape in local_shapes:
        count = 1
        for extent in shape:
            count = count * extent
        results.append(summed[offset : offset + count].reshape(shape))
        offset = offset + count
    return (
        hidden_out,
        hidden_grad,
        results[0],
        results[1],
        results[2],
        results[3],
        results[4],
        results[5],
        results[6],
        results[7],
    )


def solution(mesh):
    in_specs = (
        P("wide", "narrow", None),
        P("wide", "narrow"),
        P("wide"),
        P(),
        P(),
        P(),
        P(),
        P(),
        P(),
        P(),
        P(),
        P("wide", "narrow", None),
    )
    out_specs = (
        P("wide", "narrow", None),
        P("wide", "narrow", None),
        P("wide", "narrow"),
        P("narrow", "wide"),
        P("wide"),
        P("wide", "narrow"),
        P("wide", "narrow"),
        P("wide"),
        P("wide", "narrow"),
        P("wide", "narrow"),
    )
    return jax.shard_map(
        on_device, mesh=mesh, in_specs=in_specs, out_specs=out_specs, check_vma=False
    )
```

profile of v0, /device:TPU:0, one launch (start us, length us, event | category | flops | bytes accessed | tf_op | source)
XLA Modules:
  0.0 1036.6 jit_solution(18273378319542742261)
XLA Ops:
  10.6 5.9 copy.111
  24.7 6.3 all-to-all-start
  36.9 14.2 %all-to-all-done = bf16[2,256,768]{1,0,2:T(2,128)(2,1)S(1)} async-done(((bf16[2,256,768]{1,0,2:T(2,128)(2,1)}), bf16[2,256,768]{1,0,2:T(2,128)(2,1)S(1)}, u32[]{:S(2)}, u32[]{:S(2)}) %all-to-all-start) | async-done | bytes 786464 | tf_op jit(solution)/shard_map/all_to_all | solution.py:176
  57.5 16.7 %all-to-all-done.1 = bf16[2,256,768]{1,0,2:T(2,128)(2,1)S(1)} async-done(((bf16[2,256,768]{1,0,2:T(2,128)(2,1)}), bf16[2,256,768]{1,0,2:T(2,128)(2,1)S(1)}, u32[]{:S(2)}, u32[]{:S(2)}) %all-to-all-start.1) | async-done | bytes 786464 | tf_op jit(solution)/shard_map/all_to_all | solution.py:174
  74.2 4.7 all-to-all-start.2
  85.6 13.0 %all-to-all-done.2 = bf16[2,256,768]{1,0,2:T(2,128)(2,1)} async-done(((bf16[2,256,768]{1,0,2:T(2,128)(2,1)}), bf16[2,256,768]{1,0,2:T(2,128)(2,1)}, u32[]{:S(2)}, u32[]{:S(2)}) %all-to-all-start.2) | async-done | bytes 786464 | tf_op jit(solution)/shard_map/all_to_all | solution.py:175
  104.7 17.3 %while.26 = (s32[]{:T(128)}, bf16[2,1024,192]{1,2,0:T(8,128)(2,1)}, f32[2,3,1024,1]{2,1,3,0:T(4,128)}, bf16[2,1024,192]{1,2,0:T(8,128)(2,1)S(1)}, bf16[2,1024,19...) while((s32[]{:T(128)}, bf16[2,1024,192]{1,2,0:T(8,128)(2,1)}, ...), condition=%wide.region_5.6_spmd, body=%wide.region_2.5_spmd.sunk | while | flops 833811456 | bytes 48861340 | solution.py:178
  125.6 4.4 all-to-all-start.3
  130.1 7.9 fusion.85
  137.9 17.4 %all-to-all-done.3 = bf16[2,1024,192]{2,0,1:T(2,128)(2,1)} async-done(((bf16[2,1024,192]{2,0,1:T(2,128)(2,1)}), bf16[2,1024,192]{2,0,1:T(2,128)(2,1)}, u32[]{:S(2)}, u32[]{:S(2)}) %all-to-all-start.3) | async-done | bytes 786464 | tf_op jit(solution)/shard_map/all_to_all | solution.py:179
  164.0 12.8 %fusion.27 = (bf16[3072,512]{0,1:T(8,128)(2,1)}, bf16[3072,512]{0,1:T(8,128)(2,1)}, f32[512,3072]{1,0:T(8,128)}) fusion(f32[512,3072]{1,0:T(8,128)S(1)} %copy-done.64, bf16[512,768]{1,0:T(8,128)(2,1)S(1)} %bitcast.357, bf16[768,3072]{1,0:T(8,128)(2,1)} %param.25), kind=kOutput, calls=%fused_computation.51 | convolution fusion | flops 2450522112 | bytes 24379392 | tf_op jit(solution)/shard_map/dot_general | solution.py:191
  176.8 8.4 fusion.34
  185.3 6.3 fusion.33
  202.4 22.1 %all_to_all.114 = bf16[2,256,768]{1,0,2:T(2,128)(2,1)S(1)} all-to-all(bf16[2,256,768]{1,0,2:T(2,128)(2,1)S(1)} %copy.123), channel_id=1, replica_groups=mesh['wide'=8,'narrow'=4] {'narrow'}, dimensions={2} | all-to-all | bytes 1572864 | tf_op jit(solution)/shard_map/all_to_all | solution.py:215
  228.5 46.5 %while.27 = (s32[]{:T(128)}, bf16[2,1024,192]{1,2,0:T(8,128)(2,1)}, bf16[2,1024,192]{1,2,0:T(8,128)(2,1)}, bf16[2,1024,192]{1,2,0:T(8,128)(2,1)}, bf16[2,1024,19...) while((s32[]{:T(128)}, bf16[2,1024,192]{1,2,0:T(8,128)(2,1)}, ...), condition=%wide.region_12.13_spmd, body=%wide.region_10.12_spmd.sunk | while | flops 2051994624 | bytes 144789888 | solution.py:216
  236.0 5.3 multiply_convert_fusion.8
  259.3 5.3 multiply_convert_fusion.8
  284.3 22.7 %all-to-all-done.7 = bf16[2,1024,192]{2,0,1:T(2,128)(2,1)S(1)} async-done(((bf16[2,1024,192]{2,0,1:T(2,128)(2,1)}), bf16[2,1024,192]{2,0,1:T(2,128)(2,1)S(1)}, u32[]{:S(2)}, u32[]{:S(2)}) %all-to-all-start.7) | async-done | bytes 786464 | tf_op jit(solution)/shard_map/all_to_all | solution.py:222
  322.2 13.7 %all-to-all-done.5 = bf16[2,1024,192]{2,0,1:T(2,128)(2,1)S(1)} async-done(((bf16[2,1024,192]{2,0,1:T(2,128)(2,1)}), bf16[2,1024,192]{2,0,1:T(2,128)(2,1)S(1)}, u32[]{:S(2)}, u32[]{:S(2)}) %all-to-all-start.5) | async-done | bytes 786464 | tf_op jit(solution)/shard_map/all_to_all | solution.py:220
  348.1 4.7 copy.161
  352.7 4.5 fusion.87
  357.2 9.0 copy.168
  366.3 4.8 copy.162
  371.0 6.9 convolution_bitcast_fusion
  377.9 11.5 %copy.145 = f32[8,4,384,192]{3,2,1,0:T(8,128)} copy(f32[8,4,384,192]{2,3,1,0:T(8,128)} %convolution_bitcast_fusion) | data formatting | bytes 18874368 | tf_op jit(solution)/shard_map/transpose | solution.py:106
  389.4 11.1 %concatenate.41 = f32[32,73728]{1,0:T(8,128)} reshape(f32[8,4,384,192]{3,2,1,0:T(8,128)} %copy.145) | data formatting | bytes 18874368 | tf_op jit(solution)/shard_map/concatenate | solution.py:304
  444.8 8.6 concatenate.37
  456.3 20.7 %dynamic-update-slice.3 = f32[32,243904]{1,0:T(8,128)} dynamic-update-slice(f32[32,243904]{1,0:T(8,128)} %dynamic-update-slice.2, f32[32,55296]{1,0:T(8,128)} %concatenate.37, s32[]{} %constant.108, s32[]{} %constant.111) | dynamic-update-slice | bytes 14155780
  476.9 8.9 dynamic-update-slice.4
  487.4 28.8 %dynamic-update-slice.6 = f32[32,243904]{1,0:T(8,128)} dynamic-update-slice(f32[32,243904]{1,0:T(8,128)} %dynamic-update-slice.5, f32[32,73728]{1,0:T(8,128)} %bitcast.326, s32[]{} %constant.108, s32[]{} %constant.114) | dynamic-update-slice | bytes 18874372
  516.1 28.6 %dynamic-update-slice.7 = f32[32,243904]{1,0:T(8,128)} dynamic-update-slice(f32[32,243904]{1,0:T(8,128)} %dynamic-update-slice.6, f32[32,73728]{1,0:T(8,128)} %concatenate.41, s32[]{} %constant.108, s32[]{} %constant.115) | dynamic-update-slice | bytes 18874372 | tf_op jit(solution)/shard_map/concatenate | solution.py:304
  544.8 469.4 %all-reduce.7.cloned.1.call-done = f32[32,243904]{1,0:T(8,128)} async-done(((f32[32,243904]{1,0:T(8,128)}), f32[32,243904]{1,0:T(8,128)}) %all-reduce.7.cloned.1.call-update) | async-done | bytes 31219728
  (327 shorter events, 216.3 us)
Async XLA Ops:
  7.2 153.2 %copy-start = (bf16[768,768]{1,0:T(8,128)(2,1)S(1)}, bf16[768,768]{1,0:T(8,128)(2,1)}, u32[]{:S(2)}) copy-start(bf16[768,768]{1,0:T(8,128)(2,1)} %param.23) | copy-start | bytes 3538948
  10.6 6.6 copy-start.40
  10.6 6.6 copy-start.44
  10.6 5.9 copy-start.60
  10.6 5.9 copy-start.2
  10.6 6.6 copy-start.9
  22.9 8.1 copy-start.62
  24.7 26.4 %all-to-all-start = ((bf16[2,256,768]{1,0,2:T(2,128)(2,1)}), bf16[2,256,768]{1,0,2:T(2,128)(2,1)S(1)}, u32[]{:S(2)}, u32[]{:S(2)}) async-start(bf16[2,256,768]{1,0,2:T(2,128)(2,1)} %copy.112), calls=%async_computation | async-start | bytes 1572864 | tf_op jit(solution)/shard_map/all_to_all | solution.py:176
  51.1 23.1 %all-to-all-start.1 = ((bf16[2,256,768]{1,0,2:T(2,128)(2,1)}), bf16[2,256,768]{1,0,2:T(2,128)(2,1)S(1)}, u32[]{:S(2)}, u32[]{:S(2)}) async-start(bf16[2,256,768]{1,0,2:T(2,128)(2,1)} %copy.115), calls=%async_computation.1 | async-start | bytes 1572864 | tf_op jit(solution)/shard_map/all_to_all | solution.py:174
  74.2 24.4 %all-to-all-start.2 = ((bf16[2,256,768]{1,0,2:T(2,128)(2,1)}), bf16[2,256,768]{1,0,2:T(2,128)(2,1)}, u32[]{:S(2)}, u32[]{:S(2)}) async-start(bf16[2,256,768]{1,0,2:T(2,128)(2,1)} %copy.117), calls=%async_computation.2 | async-start | bytes 1572864 | tf_op jit(solution)/shard_map/all_to_all | solution.py:175
  122.0 8.1 copy-start.61
  125.6 29.7 %all-to-all-start.3 = ((bf16[2,1024,192]{2,0,1:T(2,128)(2,1)}), bf16[2,1024,192]{2,0,1:T(2,128)(2,1)}, u32[]{:S(2)}, u32[]{:S(2)}) async-start(bf16[2,1024,192]{2,0,1:T(2,128)(2,1)} %copy.119), calls=%async_computation.3 | async-start | bytes 2097152 | tf_op jit(solution)/shard_map/all_to_all | solution.py:179
  160.4 16.4 %slice-start.2 = ((s8[4718592]{0:T(1024)(128)(4,1)}), s8[4194304]{0:T(1024)(128)(4,1)S(1)}, s32[]{:S(2)}) async-start(s8[4718592]{0:T(1024)(128)(4,1)} %bitcast.371), calls=%async_computation.11 | async-start | bytes 8388608
  163.6 21.6 %slice-start.4 = ((s8[4718592]{0:T(1024)(128)(4,1)}), s8[4194304]{0:T(1024)(128)(4,1)S(1)}, s32[]{:S(2)}) async-start(s8[4718592]{0:T(1024)(128)(4,1)} %bitcast.373), calls=%async_computation.13 | async-start | bytes 8388608
  164.0 12.8 %copy-start.31 = (bf16[2,256,768]{2,1,0:T(8,128)(2,1)}, bf16[2,256,768]{2,1,0:T(8,128)(2,1)S(1)}, u32[]{:S(2)}) copy-start(bf16[2,256,768]{2,1,0:T(8,128)(2,1)S(1)} %add_convert_fusion.2) | copy-start | bytes 2359300
  164.0 12.8 %slice-start.3 = ((s8[4718592]{0:T(1024)(128)(4,1)}), s8[524288]{0:T(1024)(128)(4,1)S(1)}, s32[]{:S(2)}) async-start(s8[4718592]{0:T(1024)(128)(4,1)} %bitcast.371), calls=%async_computation.12 | async-start | bytes 1048576
  164.0 21.2 %slice-start.5 = ((s8[4718592]{0:T(1024)(128)(4,1)}), s8[524288]{0:T(1024)(128)(4,1)S(1)}, s32[]{:S(2)}) async-start(s8[4718592]{0:T(1024)(128)(4,1)} %bitcast.373), calls=%async_computation.14 | async-start | bytes 1048576
  275.1 7.2 copy-start.23
  278.7 28.3 %all-to-all-start.7 = ((bf16[2,1024,192]{2,0,1:T(2,128)(2,1)}), bf16[2,1024,192]{2,0,1:T(2,128)(2,1)S(1)}, u32[]{:S(2)}, u32[]{:S(2)}) async-start(bf16[2,1024,192]{2,0,1:T(2,128)(2,1)} %copy.130), calls=%async_computation.7 | async-start | bytes 2097152 | tf_op jit(solution)/shard_map/all_to_all | solution.py:222
  282.3 33.0 %copy-start.8 = (bf16[2,4,256,192]{2,1,3,0:T(4,128)(2,1)S(1)}, bf16[2,4,256,192]{2,1,3,0:T(4,128)(2,1)}, u32[]{:S(2)}) copy-start(bf16[2,4,256,192]{2,1,3,0:T(4,128)(2,1)} %copy.160) | copy-start | bytes 2359300
  307.0 28.9 %all-to-all-start.5 = ((bf16[2,1024,192]{2,0,1:T(2,128)(2,1)}), bf16[2,1024,192]{2,0,1:T(2,128)(2,1)S(1)}, u32[]{:S(2)}, u32[]{:S(2)}) async-start(bf16[2,1024,192]{2,0,1:T(2,128)(2,1)} %copy.126), calls=%async_computation.5 | async-start | bytes 2097152 | tf_op jit(solution)/shard_map/all_to_all | solution.py:220
  335.9 8.1 copy-start.16
  335.9 66.2 %all-to-all-start.6 = ((bf16[2,1024,192]{2,0,1:T(2,128)(2,1)}), bf16[2,1024,192]{2,0,1:T(2,128)(2,1)}, u32[]{:S(2)}, u32[]{:S(2)}) async-start(bf16[2,1024,192]{2,0,1:T(2,128)(2,1)} %copy.128), calls=%async_computation.6 | async-start | bytes 2097152 | tf_op jit(solution)/shard_map/all_to_all | solution.py:221
  340.1 674.1 %all-reduce.7.cloned.1.call-start = ((), (), s32[]{:S(2)}) async-start(), calls=%async_computation.8 | async-start | bytes 62455808
  366.3 4.8 copy-start.35
  389.4 11.8 %copy-start.17 = (bf16[2,1024,192]{2,0,1:T(2,128)(2,1)S(1)}, bf16[2,1024,192]{2,0,1:T(2,128)(2,1)}, u32[]{:S(2)}) copy-start(bf16[2,1024,192]{2,0,1:T(2,128)(2,1)} %copy-done.16) | copy-start | bytes 2359300
  400.5 5.4 copy-start.37
  400.5 5.4 copy-start.39
  417.4 5.1 copy-start.63
  444.8 8.6 copy-start.6
  456.2 20.7 %copy-start.7 = (f32[32,18432]{1,0:T(8,128)S(1)}, f32[32,18432]{1,0:T(8,128)}, u32[]{:S(2)}) copy-start(f32[32,18432]{1,0:T(8,128)} %concatenate.38) | copy-start | bytes 7077892
  544.7 484.5 %copy-start.1 = (bf16[768,768]{1,0:T(8,128)(2,1)S(1)}, bf16[768,768]{1,0:T(8,128)(2,1)}, u32[]{:S(2)}) copy-start(bf16[768,768]{1,0:T(8,128)(2,1)} %param.23) | copy-start | bytes 3538948
  (58 other events, 145.4 us)
Sparse Core Ops, SparseCore 0:
  544.9 469.2 all-reduce.6
where the time goes:
time: 1050 us; the launch traced here: 1040 us
  waiting for transfers between devices  567 us (54%)
  local copies, waits for them, and re-layouts  259 us (25%)
  matrix products  108 us (10%)
  other arithmetic  34.6 us (3%)
  starting transfers between devices  30.4 us (3%)
  blocking collectives  22.1 us (2%)
  between operations  15.5 us (1%)
    unnamed x2, waiting for transfers between devices  469 us
    unnamed x139, local copies, waits for them, and re-layouts  85.9 us
    concatenate x6, local copies, waits for them, and re-layouts, on_device(): stacked = jnp.concatenate(block_list, axis=2)  58.1 us
    all_to_all x1, waiting for transfers between devices, on_device(): lax.all_to_all(d_value_heads, 'narrow', split_axis=1, concat_axis=2, tile...  22.7 us
    all_to_all x1, blocking collectives, on_device(): lax.all_to_all(d_attended, 'narrow', split_axis=2, concat_axis=1, tiled=T...  22.1 us
  transfers between devices with their start and end apart: 8, of which 7 were waited for; matrix products, arithmetic and copies ran while one was open for 9% of the time, Pallas kernels for 0%

commit v1 on v0

--- a/solution.py
+++ b/solution.py
@@ -6,6 +6,22 @@
 HEAD_DIM = 64
 HIGHEST = lax.Precision.HIGHEST
 norm_eps = 1e-05
+
+
+def exchange_in_pairs(shard, axis, split, join):
+    ways, here = (lax.axis_size(axis), lax.axis_index(axis))
+    width = shard.shape[split] // ways
+    lengths = list(shard.shape)
+    lengths[split] = width
+    height = lengths[join]
+    lengths[join] = height * ways
+    full = jnp.zeros(lengths, shard.dtype)
+    for mask in range(ways):
+        part = lax.dynamic_slice_in_dim(shard, (here ^ mask) * width, width, axis=split)
+        if mask:
+            part = lax.ppermute(part, axis, [(d, d ^ mask) for d in range(ways)])
+        full = lax.dynamic_update_slice_in_dim(full, part, (here ^ mask) * height, axis=join)
+    return full
 
 
 def norm_mod(hidden, gain, shift, scale):
@@ -172,7 +188,7 @@
     value_low = qkv[:, :, 2].astype(jnp.bfloat16).reshape(row_count, part_len, model_width)
     query_heads, key_heads, value_heads = (
         lax.all_to_all(query_low, "narrow", split_axis=2, concat_axis=1, tiled=True),
-        lax.all_to_all(key_low, "narrow", split_axis=2, concat_axis=1, tiled=True),
+        exchange_in_pairs(key_low, "narrow", 2, 1),
         lax.all_to_all(value_low, "narrow", split_axis=2, concat_axis=1, tiled=True),
     )
     attended_heads, log_totals = lax.map(attend, (query_heads, key_heads, value_heads))

time: 1050 us -> 1040 us (level)
    ppermute x0 -> x3, waiting for transfers between devices: none -> 25.9 us  [exchange_in_pairs(): part = lax.ppermute(part, axis, [(d, d ^ mask) for d in range(ways)])]
    all_to_all x1, waiting for transfers between devices: 16.7 us -> 0.01 us  [on_device(): lax.all_to_all(query_low, 'narrow', split_axis=2, concat_axis=1, tiled=True)]
    all_to_all x1 -> x0, waiting for transfers between devices: 13 us -> none  [on_device(): lax.all_to_all(key_low, 'narrow', split_axis=2, concat_axis=1, tiled=True)]
    unnamed x139 -> x141, local copies, waits for them, and re-layouts: 85.9 us -> 86.9 us
  transfers between devices with their start and end apart: 8 -> 10, of which waited for: 7 -> 7; matrix products, arithmetic and copies ran while one was open for 9% -> 9% of each run, Pallas kernels for 0% -> 0%
where the time goes in v1:
time: 1040 us; the launch traced here: 1030 us
  waiting for transfers between devices  563 us (54%)
  local copies, waits for them, and re-layouts  258 us (25%)
  matrix products  108 us (10%)
  other arithmetic  34.7 us (3%)
  starting transfers between devices  31.3 us (3%)
  blocking collectives  22.7 us (2%)
  between operations  15.6 us (2%)
    unnamed x2, waiting for transfers between devices  470 us
    unnamed x141, local copies, waits for them, and re-layouts  86.9 us
    concatenate x6, local copies, waits for them, and re-layouts, on_device(): stacked = jnp.concatenate(block_list, axis=2)  58.1 us
    ppermute x3, waiting for transfers between devices, exchange_in_pairs(): part = lax.ppermute(part, axis, [(d, d ^ mask) for d in range(ways)])  25.9 us
    all_to_all x1, blocking collectives, on_device(): lax.all_to_all(d_attended, 'narrow', split_axis=2, concat_axis=1, tiled=T...  22.7 us
    all_to_all x1, waiting for transfers between devices, on_device(): lax.all_to_all(d_value_heads, 'narrow', split_axis=1, concat_axis=2, tile...  22.5 us
  transfers between devices with their start and end apart: 10, of which 7 were waited for; matrix products, arithmetic and copies ran while one was open for 9% of the time, Pallas kernels for 0%

profile of v1, /device:TPU:0, one launch (start us, length us, event | category | flops | bytes accessed | tf_op | source)
XLA Modules:
  0.0 1032.9 jit_solution(11211936486058706057)
XLA Ops:
  10.6 5.9 copy.108
  24.7 6.3 all-to-all-start
  36.9 14.2 %all-to-all-done = bf16[2,256,768]{1,0,2:T(2,128)(2,1)S(1)} async-done(((bf16[2,256,768]{1,0,2:T(2,128)(2,1)}), bf16[2,256,768]{1,0,2:T(2,128)(2,1)S(1)}, u32[]{:S(2)}, u32[]{:S(2)}) %all-to-all-start) | async-done | bytes 786464 | tf_op jit(solution)/shard_map/all_to_all | solution.py:192
  51.1 4.7 all-to-all-start.1
  62.4 11.8 %collective-permute-done = bf16[2,256,192]{1,2,0:T(8,128)(2,1)} collective-permute-done((bf16[2,256,192]{1,2,0:T(8,128)(2,1)}, bf16[2,256,192]{1,2,0:T(8,128)(2,1)}, u32[]{:S(2)}, u32[]{:S(2)}) %collective-permute-start) | collective-permute-done | bytes 196640 | tf_op jit(solution)/shard_map/ppermute | solution.py:22
  75.1 14.1 %collective-permute-done.1 = bf16[2,256,192]{1,2,0:T(8,128)(2,1)} collective-permute-done((bf16[2,256,192]{1,2,0:T(8,128)(2,1)}, bf16[2,256,192]{1,2,0:T(8,128)(2,1)}, u32[]{:S(2)}, u32[]{:S(2)}) %collective-permute-start.1) | collective-permute-done | bytes 196640 | tf_op jit(solution)/shard_map/ppermute | solution.py:22
  100.8 17.3 %while.26 = (s32[]{:T(128)}, bf16[2,1024,192]{1,2,0:T(8,128)(2,1)}, f32[2,3,1024,1]{2,1,3,0:T(4,128)}, bf16[2,1024,192]{1,2,0:T(8,128)(2,1)S(1)}, bf16[2,1024,19...) while((s32[]{:T(128)}, bf16[2,1024,192]{1,2,0:T(8,128)(2,1)}, ...), condition=%wide.region_5.6_spmd, body=%wide.region_2.5_spmd.sunk | while | flops 833811456 | bytes 48861340 | solution.py:194
  121.7 4.4 all-to-all-start.2
  126.2 7.9 fusion.85
  134.0 16.9 %all-to-all-done.2 = bf16[2,1024,192]{2,0,1:T(2,128)(2,1)} async-done(((bf16[2,1024,192]{2,0,1:T(2,128)(2,1)}), bf16[2,1024,192]{2,0,1:T(2,128)(2,1)}, u32[]{:S(2)}, u32[]{:S(2)}) %all-to-all-start.2) | async-done | bytes 786464 | tf_op jit(solution)/shard_map/all_to_all | solution.py:195
  159.7 12.8 %fusion.27 = (bf16[3072,512]{0,1:T(8,128)(2,1)}, bf16[3072,512]{0,1:T(8,128)(2,1)}, f32[512,3072]{1,0:T(8,128)}) fusion(f32[512,3072]{1,0:T(8,128)S(1)} %copy-done.65, bf16[512,768]{1,0:T(8,128)(2,1)S(1)} %bitcast.351, bf16[768,3072]{1,0:T(8,128)(2,1)} %param.25), kind=kOutput, calls=%fused_computation.51 | convolution fusion | flops 2450522112 | bytes 24379392 | tf_op jit(solution)/shard_map/dot_general | solution.py:207
  172.5 8.4 fusion.34
  180.9 6.3 fusion.33
  198.0 22.7 %all_to_all.96 = bf16[2,256,768]{1,0,2:T(2,128)(2,1)S(1)} all-to-all(bf16[2,256,768]{1,0,2:T(2,128)(2,1)S(1)} %copy.118), channel_id=1, replica_groups=mesh['wide'=8,'narrow'=4] {'narrow'}, dimensions={2} | all-to-all | bytes 1572864 | tf_op jit(solution)/shard_map/all_to_all | solution.py:231
  224.8 46.7 %while.27 = (s32[]{:T(128)}, bf16[2,1024,192]{1,2,0:T(8,128)(2,1)}, bf16[2,1024,192]{1,2,0:T(8,128)(2,1)}, bf16[2,1024,192]{1,2,0:T(8,128)(2,1)}, bf16[2,1024,19...) while((s32[]{:T(128)}, bf16[2,1024,192]{1,2,0:T(8,128)(2,1)}, ...), condition=%wide.region_12.13_spmd, body=%wide.region_10.12_spmd.sunk | while | flops 2051994624 | bytes 144789888 | solution.py:232
  232.3 5.4 multiply_convert_fusion.8
  255.7 5.4 multiply_convert_fusion.8
  280.7 22.5 %all-to-all-done.6 = bf16[2,1024,192]{2,0,1:T(2,128)(2,1)S(1)} async-done(((bf16[2,1024,192]{2,0,1:T(2,128)(2,1)}), bf16[2,1024,192]{2,0,1:T(2,128)(2,1)S(1)}, u32[]{:S(2)}, u32[]{:S(2)}) %all-to-all-start.6) | async-done | bytes 786464 | tf_op jit(solution)/shard_map/all_to_all | solution.py:238
  318.4 13.7 %all-to-all-done.4 = bf16[2,1024,192]{2,0,1:T(2,128)(2,1)S(1)} async-done(((bf16[2,1024,192]{2,0,1:T(2,128)(2,1)}), bf16[2,1024,192]{2,0,1:T(2,128)(2,1)S(1)}, u32[]{:S(2)}, u32[]{:S(2)}) %all-to-all-start.4) | async-done | bytes 786464 | tf_op jit(solution)/shard_map/all_to_all | solution.py:236
  344.3 4.7 copy.156
  349.0 4.5 fusion.87
  353.5 9.0 copy.163
  362.5 4.8 copy.157
  367.3 6.9 convolution_bitcast_fusion
  374.1 11.5 %copy.140 = f32[8,4,384,192]{3,2,1,0:T(8,128)} copy(f32[8,4,384,192]{2,3,1,0:T(8,128)} %convolution_bitcast_fusion) | data formatting | bytes 18874368 | tf_op jit(solution)/shard_map/transpose | solution.py:122
  385.6 11.1 %concatenate.41 = f32[32,73728]{1,0:T(8,128)} reshape(f32[8,4,384,192]{3,2,1,0:T(8,128)} %copy.140) | data formatting | bytes 18874368 | tf_op jit(solution)/shard_map/concatenate | solution.py:320
  441.0 8.6 concatenate.37
  452.5 20.7 %dynamic-update-slice.3 = f32[32,243904]{1,0:T(8,128)} dynamic-update-slice(f32[32,243904]{1,0:T(8,128)} %dynamic-update-slice.2, f32[32,55296]{1,0:T(8,128)} %concatenate.37, s32[]{} %constant.126, s32[]{} %constant.129) | dynamic-update-slice | bytes 14155780
  473.2 8.9 dynamic-update-slice.4
  483.6 28.8 %dynamic-update-slice.6 = f32[32,243904]{1,0:T(8,128)} dynamic-update-slice(f32[32,243904]{1,0:T(8,128)} %dynamic-update-slice.5, f32[32,73728]{1,0:T(8,128)} %bitcast.321, s32[]{} %constant.126, s32[]{} %constant.132) | dynamic-update-slice | bytes 18874372
  512.4 28.6 %dynamic-update-slice.7 = f32[32,243904]{1,0:T(8,128)} dynamic-update-slice(f32[32,243904]{1,0:T(8,128)} %dynamic-update-slice.6, f32[32,73728]{1,0:T(8,128)} %concatenate.41, s32[]{} %constant.126, s32[]{} %constant.133) | dynamic-update-slice | bytes 18874372 | tf_op jit(solution)/shard_map/concatenate | solution.py:320
  541.0 469.5 %all-reduce.7.cloned.1.call-done = f32[32,243904]{1,0:T(8,128)} async-done(((f32[32,243904]{1,0:T(8,128)}), f32[32,243904]{1,0:T(8,128)}) %all-reduce.7.cloned.1.call-update) | async-done | bytes 31219728
  (335 shorter events, 216.1 us)
Async XLA Ops:
  7.2 148.8 %copy-start = (bf16[768,768]{1,0:T(8,128)(2,1)S(1)}, bf16[768,768]{1,0:T(8,128)(2,1)}, u32[]{:S(2)}) copy-start(bf16[768,768]{1,0:T(8,128)(2,1)} %param.23) | copy-start | bytes 3538948
  10.6 6.5 copy-start.41
  10.6 6.5 copy-start.45
  10.6 5.9 copy-start.61
  10.6 5.9 copy-start.2
  10.6 6.6 copy-start.10
  22.9 8.1 copy-start.63
  24.7 26.4 %all-to-all-start = ((bf16[2,256,768]{1,0,2:T(2,128)(2,1)}), bf16[2,256,768]{1,0,2:T(2,128)(2,1)S(1)}, u32[]{:S(2)}, u32[]{:S(2)}) async-start(bf16[2,256,768]{1,0,2:T(2,128)(2,1)} %copy.109), calls=%async_computation | async-start | bytes 1572864 | tf_op jit(solution)/shard_map/all_to_all | solution.py:192
  51.1 44.3 %all-to-all-start.1 = ((bf16[2,256,768]{1,0,2:T(2,128)(2,1)}), bf16[2,256,768]{1,0,2:T(2,128)(2,1)}, u32[]{:S(2)}, u32[]{:S(2)}) async-start(bf16[2,256,768]{1,0,2:T(2,128)(2,1)} %copy.112), calls=%async_computation.1 | async-start | bytes 1572864 | tf_op jit(solution)/shard_map/all_to_all | solution.py:190
  58.0 16.2 %collective-permute-start = (bf16[2,256,192]{1,2,0:T(8,128)(2,1)}, bf16[2,256,192]{1,2,0:T(8,128)(2,1)}, u32[]{:S(2)}, u32[]{:S(2)}) collective-permute-start(bf16[2,256,192]{1,2,0:T(8,128)(2,1)} %get-tuple-element.200), channel_id=1, source_target_pairs={{0,1},{1,0},{2,3},{3,2},{4,5},{5,4},{6,7},{7,6},{8,9},{9,8},{10,11... | collective-permute-start | bytes 589832 | tf_op jit(solution)/shard_map/ppermute | solution.py:22
  60.0 29.2 %collective-permute-start.1 = (bf16[2,256,192]{1,2,0:T(8,128)(2,1)}, bf16[2,256,192]{1,2,0:T(8,128)(2,1)}, u32[]{:S(2)}, u32[]{:S(2)}) collective-permute-start(bf16[2,256,192]{1,2,0:T(8,128)(2,1)} %get-tuple-element.199), channel_id=1, source_target_pairs={{0,2},{1,3},{2,0},{3,1},{4,6},{5,7},{6,4},{7,5},{8,10},{9,11},{10,... | collective-permute-start | bytes 589832 | tf_op jit(solution)/shard_map/ppermute | solution.py:22
  62.3 27.8 %collective-permute-start.2 = (bf16[2,256,192]{1,2,0:T(8,128)(2,1)}, bf16[2,256,192]{1,2,0:T(8,128)(2,1)}, u32[]{:S(2)}, u32[]{:S(2)}) collective-permute-start(bf16[2,256,192]{1,2,0:T(8,128)(2,1)} %get-tuple-element.198), channel_id=1, source_target_pairs={{0,3},{1,2},{2,1},{3,0},{4,7},{5,6},{6,5},{7,4},{8,11},{9,10},{10,... | collective-permute-start | bytes 589832 | tf_op jit(solution)/shard_map/ppermute | solution.py:22
  118.1 8.1 copy-start.62
  121.7 29.3 %all-to-all-start.2 = ((bf16[2,1024,192]{2,0,1:T(2,128)(2,1)}), bf16[2,1024,192]{2,0,1:T(2,128)(2,1)}, u32[]{:S(2)}, u32[]{:S(2)}) async-start(bf16[2,1024,192]{2,0,1:T(2,128)(2,1)} %copy.114), calls=%async_computation.2 | async-start | bytes 2097152 | tf_op jit(solution)/shard_map/all_to_all | solution.py:195
  156.0 16.4 %slice-start.2 = ((s8[4718592]{0:T(1024)(128)(4,1)}), s8[4194304]{0:T(1024)(128)(4,1)S(1)}, s32[]{:S(2)}) async-start(s8[4718592]{0:T(1024)(128)(4,1)} %bitcast.365), calls=%async_computation.10 | async-start | bytes 8388608
  159.2 21.7 %slice-start.4 = ((s8[4718592]{0:T(1024)(128)(4,1)}), s8[4194304]{0:T(1024)(128)(4,1)S(1)}, s32[]{:S(2)}) async-start(s8[4718592]{0:T(1024)(128)(4,1)} %bitcast.367), calls=%async_computation.12 | async-start | bytes 8388608
  159.6 12.8 %copy-start.32 = (bf16[2,256,768]{2,1,0:T(8,128)(2,1)}, bf16[2,256,768]{2,1,0:T(8,128)(2,1)S(1)}, u32[]{:S(2)}) copy-start(bf16[2,256,768]{2,1,0:T(8,128)(2,1)S(1)} %add_convert_fusion.2) | copy-start | bytes 2359300
  159.6 12.8 %slice-start.3 = ((s8[4718592]{0:T(1024)(128)(4,1)}), s8[524288]{0:T(1024)(128)(4,1)S(1)}, s32[]{:S(2)}) async-start(s8[4718592]{0:T(1024)(128)(4,1)} %bitcast.365), calls=%async_computation.11 | async-start | bytes 1048576
  159.6 21.2 %slice-start.5 = ((s8[4718592]{0:T(1024)(128)(4,1)}), s8[524288]{0:T(1024)(128)(4,1)S(1)}, s32[]{:S(2)}) async-start(s8[4718592]{0:T(1024)(128)(4,1)} %bitcast.367), calls=%async_computation.13 | async-start | bytes 1048576
  271.5 7.2 copy-start.24
  275.2 28.1 %all-to-all-start.6 = ((bf16[2,1024,192]{2,0,1:T(2,128)(2,1)}), bf16[2,1024,192]{2,0,1:T(2,128)(2,1)S(1)}, u32[]{:S(2)}, u32[]{:S(2)}) async-start(bf16[2,1024,192]{2,0,1:T(2,128)(2,1)} %copy.125), calls=%async_computation.6 | async-start | bytes 2097152 | tf_op jit(solution)/shard_map/all_to_all | solution.py:238
  278.7 32.8 %copy-start.9 = (bf16[2,4,256,192]{2,1,3,0:T(4,128)(2,1)S(1)}, bf16[2,4,256,192]{2,1,3,0:T(4,128)(2,1)}, u32[]{:S(2)}) copy-start(bf16[2,4,256,192]{2,1,3,0:T(4,128)(2,1)} %copy.155) | copy-start | bytes 2359300
  303.3 28.9 %all-to-all-start.4 = ((bf16[2,1024,192]{2,0,1:T(2,128)(2,1)}), bf16[2,1024,192]{2,0,1:T(2,128)(2,1)S(1)}, u32[]{:S(2)}, u32[]{:S(2)}) async-start(bf16[2,1024,192]{2,0,1:T(2,128)(2,1)} %copy.121), calls=%async_computation.4 | async-start | bytes 2097152 | tf_op jit(solution)/shard_map/all_to_all | solution.py:236
  332.1 8.1 copy-start.17
  332.1 66.1 %all-to-all-start.5 = ((bf16[2,1024,192]{2,0,1:T(2,128)(2,1)}), bf16[2,1024,192]{2,0,1:T(2,128)(2,1)}, u32[]{:S(2)}, u32[]{:S(2)}) async-start(bf16[2,1024,192]{2,0,1:T(2,128)(2,1)} %copy.123), calls=%async_computation.5 | async-start | bytes 2097152 | tf_op jit(solution)/shard_map/all_to_all | solution.py:237
  336.4 674.1 %all-reduce.7.cloned.1.call-start = ((), (), s32[]{:S(2)}) async-start(), calls=%async_computation.7 | async-start | bytes 62455808
  385.6 11.8 %copy-start.18 = (bf16[2,1024,192]{2,0,1:T(2,128)(2,1)S(1)}, bf16[2,1024,192]{2,0,1:T(2,128)(2,1)}, u32[]{:S(2)}) copy-start(bf16[2,1024,192]{2,0,1:T(2,128)(2,1)} %copy-done.17) | copy-start | bytes 2359300
  396.7 5.4 copy-start.38
  396.7 5.4 copy-start.40
  441.0 8.6 copy-start.7
  452.5 20.7 %copy-start.8 = (f32[32,18432]{1,0:T(8,128)S(1)}, f32[32,18432]{1,0:T(8,128)}, u32[]{:S(2)}) copy-start(f32[32,18432]{1,0:T(8,128)} %concatenate.38) | copy-start | bytes 7077892
  541.0 484.5 %copy-start.1 = (bf16[768,768]{1,0:T(8,128)(2,1)S(1)}, bf16[768,768]{1,0:T(8,128)(2,1)}, u32[]{:S(2)}) copy-start(bf16[768,768]{1,0:T(8,128)(2,1)} %param.23) | copy-start | bytes 3538948
  (61 other events, 156.1 us)
Sparse Core Ops, SparseCore 0:
  541.1 469.3 all-reduce.6
